TPU v7x, 768 devices: a whole 4x8x12 slice. The times are simulated.
768 devices in a mesh: ctx: 96 (over z_lo, y, x), kvh: 8 (over z_hi, core).
Axes of the slice: x: 4, y: 8, z: 12 (z_hi: 4, z_lo: 3; z = z_hi * 3 + z_lo), core: 2. Of those that a mesh axis runs over, the one named last changes fastest.
Arguments:
- queries: float32 [96, 256, 64, 128], P('ctx', None, 'kvh'), may hold values from -64 to 64
- cache_keys: float32 [8, 49152, 128], P('kvh', 'ctx'), may hold values from -16 to 16
- cache_values: float32 [8, 49152, 128], P('kvh', 'ctx'), may hold values from -6 to 6
- bounds: int32 [96, 3], replicated, may hold values from 0 to 2048, as said below
Outputs:
- attended: float32 [96, 256, 64, 128], P('ctx', None, 'kvh')
Inputs may be any that keep to these rules, and one draw needn't show every extreme that they name: bounds[b] = (s, w, l) with 2 <= s <= 64, 0 <= w < 256, 1792 < l <= 2048; block 0 has s = 64, w = 0, l = 2048.
All inputs are finite; a program needn't handle non-finite values.
Results may differ from a plain program's by a relative error of at most 0.0003.
Values sent between devices are 32-bit elements; how exact they have to be, the bound alone decides.
A program may use at most 32 MiB of HBM per device.

v0:
```python
import math

import jax
import jax.numpy as jnp
from jax import lax
from jax.experimental import pallas as pl
from jax.experimental.pallas import tpu as pltpu
from jax.sharding import PartitionSpec as P

SINK = 64
NEG = -1e30
NT = (((1,), (1,)), ((), ()))
NN = (((1,), (0,)), ((), ()))
F32, BF16 = jnp.float32, jnp.bfloat16
XS = 4
PLANE = 32

NEAR1, TRANSIT, NEAR3, FAR_A, FAR_B, SINKS, RELAY = 0, 4, 8, 12, 14, 16, 18
SINK_SENDS = 22


def split(x):
    high = x.astype(BF16)
    return high, (x - high.astype(F32)).astype(BF16)


def kernel(rows, count, bounds, q_hbm, k_hbm, v_hbm, o_ref, q_raw, kbuf, vbuf, ksink, vsink,
           qcat, kcat, klow, vcat, top, total, mixed, ssem, rsem, lsem):
    half, queries, size = rows // 2, q_hbm.shape[0], q_hbm.shape[1]
    b = lax.axis_index("ctx")
    x = lax.rem(b, XS)
    at = lambda d: lax.rem(b + d + count, count)

    def remote(src, dst, send, recv, target):
        return pltpu.make_async_remote_copy(
            src_ref=src, dst_ref=dst, send_sem=ssem.at[send], recv_sem=rsem.at[recv],
            device_id={"ctx": target}, device_id_type=pl.DeviceIdType.MESH)

    local = [
        pltpu.make_async_copy(q_hbm, q_raw, lsem.at[0]),
        pltpu.make_async_copy(k_hbm, kbuf.at[0], lsem.at[1]),
        pltpu.make_async_copy(v_hbm, vbuf.at[0], lsem.at[2]),
    ]
    for copy in local:
        copy.start()

    barrier = pltpu.get_barrier_semaphore()
    for d in (1, -1, 3, -3, 4, -4):
        pl.semaphore_signal(barrier, inc=1, device_id={"ctx": at(d)}, device_id_type=pl.DeviceIdType.MESH)
    low = lax.rem(b, PLANE)
    sink_source = jnp.where(b < XS, 0, jnp.where(b < PLANE, x, jnp.where(low < XS, low + XS, low)))

    @pl.when(b > 0)
    def _():
        pl.semaphore_signal(barrier, inc=1, device_id={"ctx": sink_source}, device_id_type=pl.DeviceIdType.MESH)

    ys = PLANE // XS - 1
    zs = count // PLANE - 1
    sink_targets = jnp.where(
        b == 0, ys + XS - 1, jnp.where(b < XS, ys, jnp.where(b < 2 * XS, 2 * zs, jnp.where(b < PLANE, zs, 0))))
    pl.semaphore_wait(barrier, 6 + sink_targets)

    def sink_copies(from_input, number, target):
        src = (k_hbm.at[0:SINK], v_hbm.at[0:SINK]) if from_input else (ksink.at[0:SINK], vsink.at[0:SINK])
        dst = (ksink.at[0:SINK], vsink.at[0:SINK])
        return [remote(src[i], dst[i], SINK_SENDS + 2 * number + i, SINKS + i, target) for i in range(2)]

    root_sends = [c for d in range(1, XS) for c in sink_copies(True, d - 1, d)]
    root_sends += [c for d in range(1, ys + 1) for c in sink_copies(True, XS - 2 + d, d * XS)]
    head_sends = [c for d in range(1, ys + 1) for c in sink_copies(False, d - 1, b + d * XS)]
    plane_sends = [c for d in range(1, zs + 1) for c in sink_copies(False, d - 1, b + d * PLANE)]
    extra_sends = [c for d in range(1, zs + 1) for c in sink_copies(False, zs + d - 1, b + d * PLANE - XS)]
    sink_in = [remote(ksink.at[0:SINK], ksink.at[0:SINK], SINK_SENDS, SINKS, at(1)),
               remote(vsink.at[0:SINK], vsink.at[0:SINK], SINK_SENDS, SINKS + 1, at(1))]
    own_sink = [pltpu.make_async_copy(k_hbm.at[0:SINK], ksink.at[0:SINK], lsem.at[3]),
                pltpu.make_async_copy(v_hbm.at[0:SINK], vsink.at[0:SINK], lsem.at[4])]

    @pl.when(b == 0)
    def _():
        for copy in own_sink + root_sends:
            copy.start()

    first, last = x == 0, x == XS - 1
    slot1 = jnp.where(first, 4, 1)
    sem1 = jnp.where(first, TRANSIT, NEAR1)
    target1 = jnp.where(first, at(3), at(-1))
    parts = lambda slot, off: (kbuf.at[slot, pl.ds(off, half)], vbuf.at[slot, pl.ds(off, half)])
    hbm_parts = lambda off: (k_hbm.at[pl.ds(off, half)], v_hbm.at[pl.ds(off, half)])
    near1, near3, relay, far_a, far_b = [], [], [], [], []
    for h in range(2):
        for i in range(2):
            j = 2 * h + i
            off1, off3 = h * half, (1 - h) * half
            near1.append(remote(hbm_parts(off1)[i], parts(slot1, off1)[i], NEAR1 + j, sem1 + j, target1))
            near3.append(remote(hbm_parts(off3)[i], parts(3, off3)[i], NEAR3 + j, NEAR3 + j, at(-3)))
            relay.append(remote(parts(4, off1)[i], parts(1, off1)[i], RELAY + j, NEAR1 + j, at(-4)))
    for i in range(2):
        far_a.append(remote(parts(1, 0)[i], parts(2, 0)[i], FAR_A + i, FAR_A + i, at(-1)))
        far_b.append(remote(parts(3, half)[i], parts(2, half)[i], FAR_B + i, FAR_B + i, at(1)))
    for j in range(4):
        near1[j].start()
        near3[j].start()
    near1_in = [remote(parts(1, (j // 2) * half)[j % 2], parts(1, (j // 2) * half)[j % 2], NEAR1 + j, NEAR1 + j, at(-1))
                for j in range(4)]
    transit_in = [remote(parts(4, (j // 2) * half)[j % 2], parts(4, (j // 2) * half)[j % 2], NEAR1 + j, TRANSIT + j, at(-1))
                  for j in range(4)]

    for copy in local:
        copy.wait()
    scale = math.log2(math.e) / math.sqrt(size)
    step = 256

    @pl.loop(0, queries // step)
    def _(i):
        at_rows = pl.ds(pl.multiple_of(i * step, step), step)
        high, rest = split(q_raw[at_rows, :] * scale)
        qcat[at_rows, 0:size] = high
        qcat[at_rows, size:2 * size] = rest
        top[at_rows, :] = jnp.full((step, size), NEG, F32)
        total[at_rows, :] = jnp.zeros((step, size), F32)
        mixed[at_rows, :] = jnp.zeros((step, size), F32)

    ksink[SINK:, :] = jnp.zeros((128 - SINK, size), F32)
    vsink[SINK:, :] = jnp.zeros((128 - SINK, size), F32)
    sink_end, lower, upper = bounds[0, b], bounds[1, b], bounds[2, b]
    block = 512

    def piece(keys, values, bias):
        n = keys.shape[0]
        high, rest = split(keys)
        kcat[0:n, 0:size] = high
        kcat[0:n, size:2 * size] = high
        klow[0:n, :] = rest
        high, rest = split(values)
        vcat[0:n, 0:size] = high
        vcat[0:n, size:2 * size] = rest

        @pl.loop(0, queries // block)
        def _(i):
            at_rows = pl.ds(pl.multiple_of(i * block, block), block)
            q = qcat[at_rows, :]
            s = lax.dot_general(q, kcat[0:n, :], NT, preferred_element_type=F32)
            s += lax.dot_general(q[:, :size], klow[0:n, :], NT, preferred_element_type=F32)
            s += bias
            before = top[at_rows, :]
            now = jnp.maximum(before, jnp.max(s, axis=1, keepdims=True))
            decay = jnp.exp2(before - now)
            p = jnp.exp2(s - jnp.concatenate([now] * (n // 128), axis=1))
            summed = p[:, 0:128]
            for t in range(1, n // 128):
                summed = summed + p[:, t * 128:(t + 1) * 128]
            high, rest = split(p)
            out = lax.dot_general(high, vcat[0:n, :], NN, preferred_element_type=F32)
            low = lax.dot_general(rest, vcat[0:n, 0:size], NN, preferred_element_type=F32)
            top[at_rows, :] = now
            total[at_rows, :] = total[at_rows, :] * decay + summed
            mixed[at_rows, :] = mixed[at_rows, :] * decay + (out[:, :size] + out[:, size:] + low)

    @pl.loop(0, 8)
    def _(i):
        slot = jnp.where(i < 2, 0, jnp.where(i > 5, 2, jnp.where(lax.rem(i, 2) == 0, 3, 1)))
        upper_half = (i == 1) | (i == 2) | (i == 5) | (i == 6)
        off = pl.multiple_of(jnp.where(upper_half, half, 0), half)

        @pl.when((i == 1) & (b > 0) & (b < XS))
        def _():
            for copy in sink_in:
                copy.wait_recv()
            for copy in head_sends:
                copy.start()

        @pl.when(i == 2)
        def _():
            @pl.when(last)
            def _():
                transit_in[0].wait_recv()
                relay[0].start()

            for j in range(2):
                near3[j].wait_recv()
                far_b[j].start()

        @pl.when(i == 3)
        def _():
            @pl.when(last)
            def _():
                transit_in[1].wait_recv()
                relay[1].start()

            for j in range(2):
                near1_in[j].wait_recv()
                far_a[j].start()

        @pl.when(i == 4)
        def _():
            @pl.when((b >= XS) & (b < PLANE))
            def _():
                for copy in sink_in:
                    copy.wait_recv()
                for copy in plane_sends:
                    copy.start()

                @pl.when(b < 2 * XS)
                def _():
                    for copy in extra_sends:
                        copy.start()

            @pl.when(last)
            def _():
                for j in range(2, 4):
                    transit_in[j].wait_recv()
                    relay[j].start()

            for j in range(2, 4):
                near3[j].wait_recv()

        @pl.when(i == 5)
        def _():
            for j in range(2, 4):
                near1_in[j].wait_recv()

        @pl.when(i == 6)
        def _():
            for j in range(2):
                far_b[j].wait_recv()

        @pl.when(i == 7)
        def _():
            for j in range(2):
                far_a[j].wait_recv()

        offsets = slot * rows + off + lax.broadcasted_iota(jnp.int32, (1, half), 1)
        seen = (offsets >= lower) & (offsets < upper)
        piece(kbuf[slot, pl.ds(off, half), :], vbuf[slot, pl.ds(off, half), :], jnp.where(seen, 0.0, NEG))

    @pl.when(b == 0)
    def _():
        for copy in own_sink:
            copy.wait()

    @pl.when(b >= PLANE)
    def _():
        for copy in sink_in:
            copy.wait_recv()

    slots = lax.broadcasted_iota(jnp.int32, (1, 128), 1)
    place = slots - b * rows
    place = jnp.where(place < 0, place + rows * count, place)
    seen = (slots < sink_end) & jnp.logical_not((place >= lower) & (place < upper))
    piece(ksink[...], vsink[...], jnp.where(seen, 0.0, NEG))

    @pl.loop(0, queries // step)
    def _(i):
        at_rows = pl.ds(pl.multiple_of(i * step, step), step)
        o_ref[at_rows, :] = mixed[at_rows, :] / jnp.sum(total[at_rows, :], axis=1, keepdims=True)

    for copy in near1 + near3 + far_a + far_b:
        copy.wait_send()

    @pl.when(last)
    def _():
        for copy in relay:
            copy.wait_send()

    @pl.when(b == 0)
    def _():
        for copy in root_sends:
            copy.wait_send()

    @pl.when((b > 0) & (b < XS))
    def _():
        for copy in head_sends:
            copy.wait_send()

    @pl.when((b >= XS) & (b < PLANE))
    def _():
        for copy in plane_sends:
            copy.wait_send()

        @pl.when(b < 2 * XS)
        def _():
            for copy in extra_sends:
                copy.wait_send()


def solution(mesh):
    count = mesh.shape["ctx"]

    def body(queries, cache_keys, cache_values, bounds):
        shape = queries.shape
        size, rows = shape[3], cache_keys.shape[1]
        n = shape[1] * shape[2]
        vmem = pltpu.VMEM
        out = pl.pallas_call(
            lambda *refs: kernel(rows, count, *refs),
            out_shape=jax.ShapeDtypeStruct((n, size), F32),
            in_specs=[pl.BlockSpec(memory_space=pltpu.SMEM)] + [pl.BlockSpec(memory_space=pl.ANY)] * 3,
            out_specs=pl.BlockSpec(memory_space=vmem),
            scratch_shapes=[
                vmem((n, size), F32), vmem((5, rows, size), F32), vmem((5, rows, size), F32),
                vmem((128, size), F32), vmem((128, size), F32),
                vmem((n, 2 * size), BF16), vmem((rows // 2, 2 * size), BF16), vmem((rows // 2, size), BF16),
                vmem((rows // 2, 2 * size), BF16),
                vmem((n, size), F32), vmem((n, size), F32), vmem((n, size), F32),
                pltpu.SemaphoreType.DMA((SINK_SENDS + 20,)), pltpu.SemaphoreType.DMA((SINKS + 2,)),
                pltpu.SemaphoreType.DMA((5,)),
            ],
            compiler_params=pltpu.CompilerParams(collective_id=0, has_side_effects=True),
            name="attend",
        )(bounds.T, queries.reshape(n, size), cache_keys.reshape(rows, size), cache_values.reshape(rows, size))
        return out.reshape(shape)

    in_specs = (P("ctx", None, "kvh", None), P("kvh", "ctx", None), P("kvh", "ctx", None), P())
    return jax.shard_map(body, mesh=mesh, in_specs=in_specs, out_specs=P("ctx", None, "kvh", None), check_vma=False)
```

profile of v0, /device:TPU:566, one launch (start us, length us, event | category | flops | bytes accessed | tf_op | source)
XLA Modules:
  0.0 53.9 jit_solution(1062574306789141259)
XLA Ops:
  0.0 51.6 %attend.1 = f32[2048,128]{1,0:T(8,128)} custom-call(s32[3,96]{1,0:T(4,128)} %bitcast.9, f32[2048,128]{1,0:T(8,128)} %bitcast.6, f32[512,128]{1,0:T(8,128)} %bitcast.7, f32[512,128]{1,0:T(8,128)} %bitcast.8), custom_call_target="tpu_custom_call" | custom-call | tf_op jit(solution)/shard_map/attend/pallas_call | solution.py:294
  51.6 2.3 %copy.6 = f32[1,256,8,128]{3,2,1,0:T(8,128)} copy(f32[1,256,8,128]{3,2,1,0:T(8,128)} %bitcast.5) | data formatting | bytes 2097152
where the time goes:
time: 54.1 us; the launch traced here: 53.9 us
  Pallas kernels  51.6 us (95%)
  local copies, waits for them, and re-layouts  2.26 us (4%)
    pallas_call x1, Pallas kernels, body(): pl.pallas_call(lambda *refs: kernel(rows, count, *refs), out_shape=jax.Sh...  51.6 us
    unnamed x1, local copies, waits for them, and re-layouts  2.26 us

commit v1 on v0

v1 whole, which is shorter than its diff:
```python
import math

import jax
import jax.numpy as jnp
from jax import lax
from jax.experimental import pallas as pl
from jax.experimental.pallas import tpu as pltpu
from jax.sharding import PartitionSpec as P

SINK = 64
NEG = -1e30
NT = (((1,), (1,)), ((), ()))
NN = (((1,), (0,)), ((), ()))
F32, BF16 = jnp.float32, jnp.bfloat16
XS = 4
PLANE = 32

NEAR1, TRANSIT, NEAR3, FAR_A, FAR_B, SINKS, RELAY = 0, 4, 8, 12, 16, 20, 22
SINK_SENDS = 26


def split(x):
    high = x.astype(BF16)
    return high, (x - high.astype(F32)).astype(BF16)


def kernel(rows, count, bounds, q_hbm, k_hbm, v_hbm, o_ref, q_raw, kbuf, vbuf, ksink, vsink,
           qcat, kcat, vcat, top, total, mixed, s0, s1, p0, p1, d0, d1, ssem, rsem, lsem,
           wrap_ready, sink_ready):
    scores, weights, decays = (s0, s1), (p0, p1), (d0, d1)
    half, queries, size = rows // 2, q_hbm.shape[0], q_hbm.shape[1]
    b = lax.axis_index("ctx")
    x = lax.rem(b, XS)
    at = lambda d: lax.rem(b + d + count, count)

    def remote(src, dst, send, recv, target):
        return pltpu.make_async_remote_copy(
            src_ref=src, dst_ref=dst, send_sem=ssem.at[send], recv_sem=rsem.at[recv],
            device_id={"ctx": target}, device_id_type=pl.DeviceIdType.MESH)

    local = [
        pltpu.make_async_copy(q_hbm, q_raw, lsem.at[0]),
        pltpu.make_async_copy(k_hbm, kbuf.at[0], lsem.at[1]),
        pltpu.make_async_copy(v_hbm, vbuf.at[0], lsem.at[2]),
    ]
    for copy in local:
        copy.start()

    def signal(sem, target):
        pl.semaphore_signal(sem, inc=1, device_id={"ctx": target}, device_id_type=pl.DeviceIdType.MESH)

    barrier = pltpu.get_barrier_semaphore()
    ys = PLANE // XS - 1
    zs = count // PLANE - 1
    low = lax.rem(b, PLANE)
    sink_source = jnp.where(b < PLANE, x, jnp.where(low < XS, low + XS, low))
    steps = (1, 3, 4)
    for d in steps:
        signal(barrier, at(-d))

        @pl.when(b + d < count)
        def _(d=d):
            signal(barrier, at(d))

    @pl.when(b == 2)
    def _():
        signal(barrier, 0)

    @pl.when(b < XS)
    def _():
        for d in range(1, ys + 1):
            signal(barrier, b + d * XS)

    @pl.when((b >= XS) & (b < PLANE))
    def _():
        for d in range(1, zs + 1):
            signal(barrier, b + d * PLANE)

            @pl.when(b < 2 * XS)
            def _(d=d):
                signal(barrier, b + d * PLANE - XS)

    wraps = sum(jnp.where(b < d, 1, 0) for d in steps)
    extra = jnp.where((b == 0) | (b >= XS), 1, 0)
    pl.semaphore_wait(barrier, 6 - wraps + extra)

    for d in steps:
        @pl.when(b + d >= count)
        def _(d=d):
            signal(wrap_ready, at(d))

    @pl.when(b >= XS)
    def _():
        signal(sink_ready, sink_source)

    def sink_copies(from_input, number, target):
        src = (k_hbm.at[0:SINK], v_hbm.at[0:SINK]) if from_input else (ksink.at[0:SINK], vsink.at[0:SINK])
        dst = (ksink.at[0:SINK], vsink.at[0:SINK])
        return [remote(src[i], dst[i], SINK_SENDS + 2 * number + i, SINKS + i, target) for i in range(2)]

    root_sends = [c for d in range(1, XS) for c in sink_copies(True, d - 1, d)]
    row_sends = [c for d in range(1, ys + 1) for c in sink_copies(True, XS - 2 + d, d * XS)]
    head_sends = [c for d in range(1, ys + 1) for c in sink_copies(False, d - 1, b + d * XS)]
    plane_sends = [c for d in range(1, zs + 1) for c in sink_copies(False, d - 1, b + d * PLANE)]
    extra_sends = [c for d in range(1, zs + 1) for c in sink_copies(False, zs + d - 1, b + d * PLANE - XS)]
    sink_in = [remote(ksink.at[0:SINK], ksink.at[0:SINK], SINK_SENDS, SINKS, at(1)),
               remote(vsink.at[0:SINK], vsink.at[0:SINK], SINK_SENDS, SINKS + 1, at(1))]
    own_sink = [pltpu.make_async_copy(k_hbm.at[0:SINK], ksink.at[0:SINK], lsem.at[3]),
                pltpu.make_async_copy(v_hbm.at[0:SINK], vsink.at[0:SINK], lsem.at[4])]

    @pl.when(b == 0)
    def _():
        for copy in own_sink + root_sends:
            copy.start()

    first, last = x == 0, x == XS - 1
    slot1 = jnp.where(first, 4, 1)
    sem1 = jnp.where(first, TRANSIT, NEAR1)
    target1 = jnp.where(first, at(3), at(-1))
    parts = lambda slot, off: (kbuf.at[slot, pl.ds(off, half)], vbuf.at[slot, pl.ds(off, half)])
    hbm_parts = lambda off: (k_hbm.at[pl.ds(off, half)], v_hbm.at[pl.ds(off, half)])
    near1, near3, relay, far_a, far_b = [], [], [], [], []
    for h in range(2):
        for i in range(2):
            j = 2 * h + i
            off1, off3 = h * half, (1 - h) * half
            near1.append(remote(hbm_parts(off1)[i], parts(slot1, off1)[i], NEAR1 + j, sem1 + j, target1))
            near3.append(remote(hbm_parts(off3)[i], parts(3, off3)[i], NEAR3 + j, NEAR3 + j, at(-3)))
            relay.append(remote(parts(4, off1)[i], parts(1, off1)[i], RELAY + j, NEAR1 + j, at(-4)))
    quarter = half // 2
    for j in range(4):
        buf, off = (kbuf, vbuf)[j % 2], (j // 2) * quarter
        low_rows, high_rows = pl.ds(off, quarter), pl.ds(half + off, quarter)
        far_a.append(remote(buf.at[1, low_rows], buf.at[2, low_rows], FAR_A + j, FAR_A + j, at(-1)))
        far_b.append(remote(buf.at[3, high_rows], buf.at[2, high_rows], FAR_B + j, FAR_B + j, at(1)))
    for j in range(4):
        near1[j].start()

    @pl.when(b >= XS - 1)
    def _():
        for copy in near3:
            copy.start()

    near1_in = [remote(parts(1, (j // 2) * half)[j % 2], parts(1, (j // 2) * half)[j % 2], NEAR1 + j, NEAR1 + j, at(-1))
                for j in range(4)]
    transit_in = [remote(parts(4, (j // 2) * half)[j % 2], parts(4, (j // 2) * half)[j % 2], NEAR1 + j, TRANSIT + j, at(-1))
                  for j in range(4)]

    for copy in local:
        copy.wait()
    scale = math.log2(math.e) / math.sqrt(size)
    step = 256
    lane = lax.broadcasted_iota(jnp.int32, (step, size), 1)

    @pl.loop(0, queries // step)
    def _(i):
        at_rows = pl.ds(pl.multiple_of(i * step, step), step)
        high, rest = split(q_raw[at_rows, :] * scale)
        qcat[at_rows, 0:size] = high
        qcat[at_rows, size:2 * size] = rest
        qcat[at_rows, 2 * size:3 * size] = high
        qcat[at_rows, 3 * size:4 * size] = jnp.where(lane == 0, 1.0, 0.0).astype(BF16)
        top[at_rows, :] = jnp.full((step, size), NEG, F32)
        total[at_rows, :] = jnp.zeros((step, size), F32)
        mixed[at_rows, :] = jnp.zeros((step, size), F32)

    ksink[SINK:, :] = jnp.zeros((half - SINK, size), F32)
    vsink[SINK:, :] = jnp.zeros((half - SINK, size), F32)
    sink_end, lower, upper = bounds[0, b], bounds[1, b], bounds[2, b]
    block = 512
    tiles = queries // block

    def prepare(side, keys, values, seen):
        high, rest = split(keys)
        kcat[side, :, 0:size] = high
        kcat[side, :, size:2 * size] = high
        kcat[side, :, 2 * size:3 * size] = rest
        bias = jnp.where(seen & (lax.broadcasted_iota(jnp.int32, (half, size), 1) == 0), NEG, 0.0)
        kcat[side, :, 3 * size:4 * size] = bias.astype(BF16)
        high, rest = split(values)
        vcat[side, 0:half, 0:size] = high
        vcat[side, 0:half, size:2 * size] = rest
        vcat[side, half:2 * half, 0:size] = high
        vcat[side, half:2 * half, size:2 * size] = rest

    def rows_of(t):
        return pl.ds(pl.multiple_of(lax.rem(t, tiles) * block, block), block)

    def side_of(t):
        return lax.rem(lax.div(t, tiles), 2)

    def score(t, even):
        scores[even][...] = lax.dot_general(qcat[rows_of(t), :], kcat[side_of(t)], NT, preferred_element_type=F32)

    def soften(t, even):
        s = scores[even][...]
        at_rows = rows_of(t)
        before = top[at_rows, :]
        now = jnp.maximum(before, jnp.max(s, axis=1, keepdims=True))
        decay = jnp.exp2(before - now)
        p = jnp.exp2(s - jnp.concatenate([now] * (half // 128), axis=1))
        summed = p[:, 0:128]
        for c in range(1, half // 128):
            summed = summed + p[:, c * 128:(c + 1) * 128]
        high, rest = split(p)
        weights[even][:, 0:half] = high
        weights[even][:, half:2 * half] = rest
        decays[even][...] = decay
        top[at_rows, :] = now
        total[at_rows, :] = total[at_rows, :] * decay + summed

    def mix(t, even):
        out = lax.dot_general(weights[even][...], vcat[side_of(t)], NN, preferred_element_type=F32)
        at_rows = rows_of(t)
        mixed[at_rows, :] = mixed[at_rows, :] * decays[even][...] + (out[:, :size] + out[:, size:])

    def pair(t):
        for u in range(2):
            mix(t + u - 2, u)
            soften(t + u - 1, 1 - u)
            score(t + u, u)

    pieces = 9

    def unseen(offsets):
        return (offsets < lower) | (offsets >= upper)

    slots = lax.broadcasted_iota(jnp.int32, (half, size), 0)
    prepare(0, kbuf[0, 0:half, :], vbuf[0, 0:half, :], unseen(slots))
    score(0, 0)
    score(1, 1)
    soften(0, 0)
    pair(2)

    @pl.loop(1, pieces)
    def _(i):
        slot = jnp.where(i < 2, 0, jnp.where(i > 5, 2, jnp.where(lax.rem(i, 2) == 0, 3, 1)))
        upper_half = (i == 1) | (i == 2) | (i == 5)
        off = pl.multiple_of(jnp.where(upper_half, half, jnp.where(i == 7, quarter, 0)), quarter)
        next_off = pl.multiple_of(off + jnp.where(i > 5, half, quarter), quarter)

        @pl.when((i == 1) & (b < XS - 1))
        def _():
            pl.semaphore_wait(wrap_ready, wraps)
            for copy in near3:
                copy.start()

        @pl.when((i == 1) & (b == 0))
        def _():
            pl.semaphore_wait(sink_ready, ys)
            for copy in row_sends:
                copy.start()

        @pl.when(i == 2)
        def _():
            @pl.when(b == XS - 1)
            def _():
                pl.semaphore_wait(wrap_ready, 1)

            @pl.when(last)
            def _():
                transit_in[0].wait_recv()
                relay[0].start()

            for j in range(2):
                near3[j].wait_recv()
            for copy in far_b:
                copy.start()

            @pl.when(last)
            def _():
                transit_in[1].wait_recv()
                relay[1].start()

            @pl.when((b > 0) & (b < XS))
            def _():
                for copy in sink_in:
                    copy.wait_recv()
                pl.semaphore_wait(sink_ready, ys)
                for copy in head_sends:
                    copy.start()

        @pl.when(i == 3)
        def _():
            @pl.when(last)
            def _():
                for j in range(2, 4):
                    transit_in[j].wait_recv()
                    relay[j].start()

            for j in range(2):
                near1_in[j].wait_recv()
            for copy in far_a:
                copy.start()

        @pl.when(i == 4)
        def _():
            for j in range(2, 4):
                near3[j].wait_recv()

        @pl.when(i == 5)
        def _():
            for j in range(2, 4):
                near1_in[j].wait_recv()

        row = lax.div(b, XS)
        turn = jnp.where(row == 1, 4, 5)

        @pl.when((i == turn) & (b >= XS) & (b < PLANE))
        def _():
            for copy in sink_in:
                copy.wait_recv()
            pl.semaphore_wait(sink_ready, jnp.where(row == 1, 2 * zs, zs))
            for copy in plane_sends:
                copy.start()

            @pl.when(row == 1)
            def _():
                for copy in extra_sends:
                    copy.start()

        @pl.when(i == 6)
        def _():
            for j in range(2):
                far_b[j].wait_recv()
                far_a[j].wait_recv()

        @pl.when(i == 7)
        def _():
            for j in range(2, 4):
                far_b[j].wait_recv()
                far_a[j].wait_recv()

        @pl.when(i < pieces - 1)
        def _():
            both = lambda buf: jnp.concatenate(
                [buf[slot, pl.ds(off, quarter), :], buf[slot, pl.ds(next_off, quarter), :]], axis=0)
            offsets = slot * rows + slots + jnp.where(slots < quarter, off, next_off - quarter)
            prepare(lax.rem(i, 2), both(kbuf), both(vbuf), unseen(offsets))

        @pl.when(i == pieces - 1)
        def _():
            @pl.when(b == 0)
            def _():
                for copy in own_sink:
                    copy.wait()

            @pl.when(b >= PLANE)
            def _():
                for copy in sink_in:
                    copy.wait_recv()

            place = slots - b * rows
            place = jnp.where(place < 0, place + rows * count, place)
            prepare((pieces - 1) % 2, ksink[...], vsink[...], (slots >= sink_end) | jnp.logical_not(unseen(place)))

        @pl.loop(0, tiles // 2)
        def _(c):
            pair(i * tiles + 2 * c)

    last_tile = pieces * tiles - 1
    mix(last_tile - 1, 0)
    soften(last_tile, 1)
    mix(last_tile, 1)

    @pl.loop(0, queries // step)
    def _(i):
        at_rows = pl.ds(pl.multiple_of(i * step, step), step)
        o_ref[at_rows, :] = mixed[at_rows, :] / jnp.sum(total[at_rows, :], axis=1, keepdims=True)

    for copy in near1 + near3 + far_a + far_b:
        copy.wait_send()

    @pl.when(last)
    def _():
        for copy in relay:
            copy.wait_send()

    @pl.when(b == 0)
    def _():
        for copy in root_sends + row_sends:
            copy.wait_send()

    @pl.when((b > 0) & (b < XS))
    def _():
        for copy in head_sends:
            copy.wait_send()

    @pl.when((b >= XS) & (b < PLANE))
    def _():
        for copy in plane_sends:
            copy.wait_send()

        @pl.when(b < 2 * XS)
        def _():
            for copy in extra_sends:
                copy.wait_send()


def solution(mesh):
    count = mesh.shape["ctx"]

    def body(queries, cache_keys, cache_values, bounds):
        shape = queries.shape
        size, rows = shape[3], cache_keys.shape[1]
        n = shape[1] * shape[2]
        vmem = pltpu.VMEM
        out = pl.pallas_call(
            lambda *refs: kernel(rows, count, *refs),
            out_shape=vmem((n, size), F32),
            in_specs=[pl.BlockSpec(memory_space=pltpu.SMEM)] + [pl.BlockSpec(memory_space=pl.ANY)] * 3,
            out_specs=pl.BlockSpec(memory_space=vmem),
            scratch_shapes=[
                vmem((n, size), F32), vmem((5, rows, size), F32), vmem((5, rows, size), F32),
                vmem((rows // 2, size), F32), vmem((rows // 2, size), F32),
                vmem((n, 4 * size), BF16), vmem((2, rows // 2, 4 * size), BF16), vmem((2, rows, 2 * size), BF16),
                vmem((n, size), F32), vmem((n, size), F32), vmem((n, size), F32),
                vmem((512, rows // 2), F32), vmem((512, rows // 2), F32),
                vmem((512, rows), BF16), vmem((512, rows), BF16), vmem((512, size), F32), vmem((512, size), F32),
                pltpu.SemaphoreType.DMA((SINK_SENDS + 20,)), pltpu.SemaphoreType.DMA((SINKS + 2,)),
                pltpu.SemaphoreType.DMA((5,)), pltpu.SemaphoreType.REGULAR, pltpu.SemaphoreType.REGULAR,
            ],
            compiler_params=pltpu.CompilerParams(collective_id=0, has_side_effects=True),
            name="attend",
        )(bounds.T, queries.reshape(n, size), cache_keys.reshape(rows, size), cache_values.reshape(rows, size))
        return out.reshape(shape)

    in_specs = (P("ctx", None, "kvh", None), P("kvh", "ctx", None), P("kvh", "ctx", None), P())
    return jax.shard_map(body, mesh=mesh, in_specs=in_specs, out_specs=P("ctx", None, "kvh", None), check_vma=False)
```

time: 54.1 us -> 41.1 us (0.76)
  the two profiles are of different devices: /device:TPU:566 before, /device:TPU:510 now
where the time goes in v1:
time: 41.1 us; the launch traced here: 40.9 us
  Pallas kernels  39.9 us (97%)
  local copies, waits for them, and re-layouts  0.97 us (2%)
    pallas_call x1, Pallas kernels, body(): pl.pallas_call(lambda *refs: kernel(rows, count, *refs), out_shape=vmem((...  39.9 us
    unnamed x1, local copies, waits for them, and re-layouts  0.97 us

profile of v1, /device:TPU:510, one launch (start us, length us, event | category | flops | bytes accessed | tf_op | source)
XLA Modules:
  0.0 40.9 jit_solution(6281126326401138941)
XLA Ops:
  0.0 39.9 %attend.1 = f32[2048,128]{1,0:T(8,128)S(1)} custom-call(s32[3,96]{1,0:T(4,128)} %bitcast.9, f32[2048,128]{1,0:T(8,128)} %bitcast.6, f32[512,128]{1,0:T(8,128)} %bitcast.7, f32[512,128]{1,0:T(8,128)} %bitcast.8), custom_call_target="tpu_custom_call" | custom-call | tf_op jit(solution)/shard_map/attend/pallas_call | solution.py:408
  39.9 1.0 %copy.6 = f32[1,256,8,128]{3,2,1,0:T(8,128)} copy(f32[1,256,8,128]{3,2,1,0:T(8,128)S(1)} %bitcast.5) | data formatting | bytes 2097152

commit v2 on v1

--- a/solution.py
+++ b/solution.py
@@ -53,7 +53,9 @@
     ys = PLANE // XS - 1
     zs = count // PLANE - 1
     low = lax.rem(b, PLANE)
-    sink_source = jnp.where(b < PLANE, x, jnp.where(low < XS, low + XS, low))
+    mid_row = PLANE // XS // 2
+    mid = mid_row * XS
+    sink_source = jnp.where(b < PLANE, jnp.where((x == 0) & (b > mid), mid, x), jnp.where(low < XS, low + XS, low))
     steps = (1, 3, 4)
     for d in steps:
         signal(barrier, at(-d))
@@ -69,6 +71,13 @@
     @pl.when(b < XS)
     def _():
         for d in range(1, ys + 1):
+            @pl.when((b > 0) | (d <= mid_row))
+            def _(d=d):
+                signal(barrier, b + d * XS)
+
+    @pl.when(b == mid)
+    def _():
+        for d in range(1, ys - mid_row + 1):
             signal(barrier, b + d * XS)
 
     @pl.when((b >= XS) & (b < PLANE))
@@ -99,7 +108,8 @@
         return [remote(src[i], dst[i], SINK_SENDS + 2 * number + i, SINKS + i, target) for i in range(2)]
 
     root_sends = [c for d in range(1, XS) for c in sink_copies(True, d - 1, d)]
-    row_sends = [c for d in range(1, ys + 1) for c in sink_copies(True, XS - 2 + d, d * XS)]
+    row_sends = [c for d in range(mid_row, 0, -1) for c in sink_copies(True, XS - 2 + d, d * XS)]
+    mid_sends = [c for d in range(1, ys - mid_row + 1) for c in sink_copies(False, 2 * zs + d - 1, b + d * XS)]
     head_sends = [c for d in range(1, ys + 1) for c in sink_copies(False, d - 1, b + d * XS)]
     plane_sends = [c for d in range(1, zs + 1) for c in sink_copies(False, d - 1, b + d * PLANE)]
     extra_sends = [c for d in range(1, zs + 1) for c in sink_copies(False, zs + d - 1, b + d * PLANE - XS)]
@@ -234,21 +244,23 @@
 
     @pl.loop(1, pieces)
     def _(i):
-        slot = jnp.where(i < 2, 0, jnp.where(i > 5, 2, jnp.where(lax.rem(i, 2) == 0, 3, 1)))
-        upper_half = (i == 1) | (i == 2) | (i == 5)
-        off = pl.multiple_of(jnp.where(upper_half, half, jnp.where(i == 7, quarter, 0)), quarter)
-        next_off = pl.multiple_of(off + jnp.where(i > 5, half, quarter), quarter)
+        k = jnp.where(b == 0, jnp.where(i == 5, 8, jnp.where(i == 7, 5, jnp.where(i == 8, 7, i))), i)
+        far = (k == 5) | (k == 7)
+        slot = jnp.where(k < 2, 0, jnp.where(far, 2, jnp.where((k == 2) | (k == 6), 3, 1)))
+        upper_half = (k == 1) | (k == 2) | (k == 4)
+        off = pl.multiple_of(jnp.where(upper_half, half, jnp.where(k == 7, quarter, 0)), quarter)
+        next_off = pl.multiple_of(off + jnp.where(far, half, quarter), quarter)
+
+        @pl.when((i == 1) & (b == 0))
+        def _():
+            pl.semaphore_wait(sink_ready, mid_row)
+            for copy in row_sends:
+                copy.start()
 
         @pl.when((i == 1) & (b < XS - 1))
         def _():
             pl.semaphore_wait(wrap_ready, wraps)
             for copy in near3:
-                copy.start()
-
-        @pl.when((i == 1) & (b == 0))
-        def _():
-            pl.semaphore_wait(sink_ready, ys)
-            for copy in row_sends:
                 copy.start()
 
         @pl.when(i == 2)
@@ -293,52 +305,62 @@
             for copy in far_a:
                 copy.start()
 
+            @pl.when(b == mid)
+            def _():
+                for copy in sink_in:
+                    copy.wait_recv()
+                pl.semaphore_wait(sink_ready, ys - mid_row + zs)
+                for copy in mid_sends:
+                    copy.start()
+
+        row = lax.div(b, XS)
+
+        @pl.when((i == jnp.where(row == 1, 4, 5)) & (b >= XS) & (b < PLANE))
+        def _():
+            @pl.when(b != mid)
+            def _():
+                for copy in sink_in:
+                    copy.wait_recv()
+                pl.semaphore_wait(sink_ready, jnp.where(row == 1, 2 * zs, zs))
+
+            for copy in plane_sends:
+                copy.start()
+
+            @pl.when(row == 1)
+            def _():
+                for copy in extra_sends:
+                    copy.start()
+
         @pl.when(i == 4)
-        def _():
-            for j in range(2, 4):
-                near3[j].wait_recv()
-
-        @pl.when(i == 5)
         def _():
             for j in range(2, 4):
                 near1_in[j].wait_recv()
 
-        row = lax.div(b, XS)
-        turn = jnp.where(row == 1, 4, 5)
-
-        @pl.when((i == turn) & (b >= XS) & (b < PLANE))
-        def _():
-            for copy in sink_in:
-                copy.wait_recv()
-            pl.semaphore_wait(sink_ready, jnp.where(row == 1, 2 * zs, zs))
-            for copy in plane_sends:
-                copy.start()
-
-            @pl.when(row == 1)
-            def _():
-                for copy in extra_sends:
-                    copy.start()
-
-        @pl.when(i == 6)
+        @pl.when(k == 5)
         def _():
             for j in range(2):
                 far_b[j].wait_recv()
                 far_a[j].wait_recv()
 
-        @pl.when(i == 7)
+        @pl.when(k == 6)
+        def _():
+            for j in range(2, 4):
+                near3[j].wait_recv()
+
+        @pl.when(k == 7)
         def _():
             for j in range(2, 4):
                 far_b[j].wait_recv()
                 far_a[j].wait_recv()
 
-        @pl.when(i < pieces - 1)
+        @pl.when(k < pieces - 1)
         def _():
             both = lambda buf: jnp.concatenate(
                 [buf[slot, pl.ds(off, quarter), :], buf[slot, pl.ds(next_off, quarter), :]], axis=0)
             offsets = slot * rows + slots + jnp.where(slots < quarter, off, next_off - quarter)
             prepare(lax.rem(i, 2), both(kbuf), both(vbuf), unseen(offsets))
 
-        @pl.when(i == pieces - 1)
+        @pl.when(k == pieces - 1)
         def _():
             @pl.when(b == 0)
             def _():
@@ -352,7 +374,7 @@
 
             place = slots - b * rows
             place = jnp.where(place < 0, place + rows * count, place)
-            prepare((pieces - 1) % 2, ksink[...], vsink[...], (slots >= sink_end) | jnp.logical_not(unseen(place)))
+            prepare(lax.rem(i, 2), ksink[...], vsink[...], (slots >= sink_end) | jnp.logical_not(unseen(place)))
 
         @pl.loop(0, tiles // 2)
         def _(c):
@@ -379,6 +401,11 @@
     @pl.when(b == 0)
     def _():
         for copy in root_sends + row_sends:
+            copy.wait_send()
+
+    @pl.when(b == mid)
+    def _():
+        for copy in mid_sends:
             copy.wait_send()
 
     @pl.when((b > 0) & (b < XS))

time: 41.1 us -> 41.8 us (1.017)
  Pallas kernels: 39.9 us -> 40.6 us
    pallas_call x1, Pallas kernels: 39.9 us -> 40.6 us  [body(): pl.pallas_call(lambda *refs: kernel(rows, count, *refs), out_shape=vmem((...]
where the time goes in v2:
time: 41.8 us; the launch traced here: 41.6 us
  Pallas kernels  40.6 us (97%)
  local copies, waits for them, and re-layouts  0.97 us (2%)
    pallas_call x1, Pallas kernels, body(): pl.pallas_call(lambda *refs: kernel(rows, count, *refs), out_shape=vmem((...  40.6 us
    unnamed x1, local copies, waits for them, and re-layouts  0.97 us

profile of v2, /device:TPU:510, one launch (start us, length us, event | category | flops | bytes accessed | tf_op | source)
XLA Modules:
  0.0 41.6 jit_solution(1656321797608871382)
XLA Ops:
  0.0 40.6 %attend.1 = f32[2048,128]{1,0:T(8,128)S(1)} custom-call(s32[3,96]{1,0:T(4,128)} %bitcast.9, f32[2048,128]{1,0:T(8,128)} %bitcast.6, f32[512,128]{1,0:T(8,128)} %bitcast.7, f32[512,128]{1,0:T(8,128)} %bitcast.8), custom_call_target="tpu_custom_call" | custom-call | tf_op jit(solution)/shard_map/attend/pallas_call | solution.py:435
  40.7 1.0 %copy.6 = f32[1,256,8,128]{3,2,1,0:T(8,128)} copy(f32[1,256,8,128]{3,2,1,0:T(8,128)S(1)} %bitcast.5) | data formatting | bytes 2097152
